TPU v7x, 32 devices: a whole 2x2x4 slice. The times are simulated.
32 devices in a mesh: seq: 8 (over z, y), head: 4 (over x, core).
Axes of the slice: x: 2, y: 2, z: 4, core: 2. Of those that a mesh axis runs over, the one named last changes fastest.
Arguments:
- queries: bfloat16 [8192, 512], P(('seq', 'head')), may hold values from -6 to 6
- key_rows: bfloat16 [8192, 128], P(('seq', 'head')), may hold values from -6 to 6
- value_rows: bfloat16 [8192, 128], P(('seq', 'head')), may hold values from -6 to 6
- out_grad: bfloat16 [8192, 512], P(('seq', 'head')), may hold values from -6 to 6
- doc_start: int32 [32], replicated, may hold values from 0 to 255
Outputs:
- outputs: bfloat16 [8192, 512], P(('seq', 'head'))
- query_grad: bfloat16 [8192, 512], P(('seq', 'head'))
- key_grad: bfloat16 [8192, 128], P(('seq', 'head'))
- value_grad: bfloat16 [8192, 128], P(('seq', 'head'))
Inputs may be any that keep to these rules, and one draw needn't show every extreme that they name: doc_start[c] is the position within span c of the first token of a new document.
All inputs are finite; a program needn't handle non-finite values.
Results may differ from a plain program's by a relative error of at most 0.0065.
Values may be sent and summed in bfloat16 or wider, within the bound.
No kernel may reach another device: no remote copies, remote signals or barrier semaphores. Data moves between devices by JAX's collectives and lax.ppermute only.
A program may use at most 128 MiB of HBM per device.

v0:
```python
import math
import jax
import jax.numpy as jnp
from jax import lax
from jax.sharding import PartitionSpec as P

HD = 128
GROUP = 4
SPANS_DEV = 4
masked_fill = -1e30


def passed_along(value, axis, steps):
    count = lax.axis_size(axis)
    first, last = (max(0, -steps), min(count, count - steps))
    return lax.ppermute(value, axis, [(source, source + steps) for source in range(first, last)])


def allowed_mask(
    first_row, row_count, key_count, halo_len, span_len, span_start, prev_begin, span_index
):
    row_pos = first_row + lax.broadcasted_iota(jnp.int32, (row_count, key_count), 0)
    col_pos = lax.broadcasted_iota(jnp.int32, (row_count, key_count), 1) - halo_len
    return (
        (col_pos <= row_pos)
        & ((col_pos >= span_start) | (span_start > row_pos))
        & (col_pos >= prev_begin - span_len)
        & ((col_pos >= 0) | (span_index > 0))
    )


def attend(query_rows, grad_rows, key_block, value_block, allowed, head_dim):
    score_scale = 1.0 / math.sqrt(head_dim)
    contract = (((2,), (2,)), ((0,), (0,)))
    forward = (((2,), (1,)), ((0,), (0,)))
    backward = (((1,), (1,)), ((0,), (0,)))
    scores = (
        lax.dot_general(query_rows, key_block, contract, preferred_element_type=jnp.float32)
        * score_scale
    )
    masked = jnp.where(allowed, scores, masked_fill)
    row_max = jnp.max(masked, axis=2, keepdims=True)
    exp_scores = jnp.where(allowed, jnp.exp(masked - row_max), 0.0)
    weights = exp_scores / jnp.sum(exp_scores, axis=2, keepdims=True)
    weights_low = weights.astype(jnp.bfloat16)
    result = lax.dot_general(
        weights_low, value_block, forward, preferred_element_type=jnp.float32
    ).astype(jnp.bfloat16)
    grad_weights = lax.dot_general(
        grad_rows, value_block, contract, preferred_element_type=jnp.float32
    )
    row_delta = jnp.sum(weights * grad_weights, axis=2, keepdims=True)
    grad_scores = (weights * (grad_weights - row_delta) * score_scale).astype(jnp.bfloat16)
    grad_query = lax.dot_general(
        grad_scores, key_block, forward, preferred_element_type=jnp.float32
    )
    grad_key = lax.dot_general(
        grad_scores, query_rows, backward, preferred_element_type=jnp.float32
    )
    grad_value = lax.dot_general(
        weights_low, grad_rows, backward, preferred_element_type=jnp.float32
    )
    return (result, grad_query, grad_key, grad_value)


def per_device(queries, key_rows, value_rows, out_grad, doc_start):
    tok_count = queries.shape[0]
    head_count = lax.axis_size("head")
    group_rows = tok_count * head_count
    span_len = group_rows // SPANS_DEV
    halo_len = span_len // 4
    half_len = span_len // 2
    rest_len = span_len - halo_len
    head_q, head_grad = (
        lax.all_to_all(queries, "head", split_axis=1, concat_axis=0, tiled=True),
        lax.all_to_all(out_grad, "head", split_axis=1, concat_axis=0, tiled=True),
    )
    full_k, full_v = (
        lax.all_gather(key_rows, "head", axis=0, tiled=True),
        lax.all_gather(value_rows, "head", axis=0, tiled=True),
    )
    column = lax.axis_index("head") // GROUP * HD
    head_k = lax.dynamic_slice_in_dim(full_k, column, HD, 1)
    head_v = lax.dynamic_slice_in_dim(full_v, column, HD, 1)
    query_3 = head_q.reshape(SPANS_DEV, span_len, HD)
    grad_3 = head_grad.reshape(SPANS_DEV, span_len, HD)
    keys_3 = head_k.reshape(SPANS_DEV, span_len, HD)
    values_3 = head_v.reshape(SPANS_DEV, span_len, HD)
    tail_k = keys_3[:, rest_len:]
    tail_v = values_3[:, rest_len:]
    edge_last_k, edge_last_v = passed_along(
        (tail_k[SPANS_DEV - 1], tail_v[SPANS_DEV - 1]), "seq", 1
    )
    edge_k = jnp.concatenate([edge_last_k[None], tail_k[: SPANS_DEV - 1]], axis=0)
    edge_v = jnp.concatenate([edge_last_v[None], tail_v[: SPANS_DEV - 1]], axis=0)
    key_block = jnp.concatenate([edge_k, keys_3], axis=1)
    value_block = jnp.concatenate([edge_v, values_3], axis=1)
    first_span = lax.axis_index("seq") * SPANS_DEV
    span_starts = lax.dynamic_slice_in_dim(doc_start, first_span, SPANS_DEV)
    before_start = lax.dynamic_slice_in_dim(doc_start, jnp.maximum(first_span - 1, 0), 1)
    prev_starts = jnp.concatenate([before_start, span_starts[: SPANS_DEV - 1]], axis=0)
    span_ids = first_span + jnp.arange(SPANS_DEV, dtype=jnp.int32)
    span_starts = span_starts.reshape(SPANS_DEV, 1, 1)
    prev_starts = prev_starts.reshape(SPANS_DEV, 1, 1)
    span_ids = span_ids.reshape(SPANS_DEV, 1, 1)
    grad_key = jnp.zeros((SPANS_DEV, halo_len + span_len, HD), jnp.float32)
    grad_value = jnp.zeros((SPANS_DEV, halo_len + span_len, HD), jnp.float32)
    results = []
    query_grads = []
    for block_index in range(2):
        first_row = block_index * half_len
        key_count = halo_len + first_row + half_len
        allowed = allowed_mask(
            first_row, half_len, key_count, halo_len, span_len, span_starts, prev_starts, span_ids
        )
        result, grad_query, part_key, part_value = attend(
            query_3[:, first_row : first_row + half_len],
            grad_3[:, first_row : first_row + half_len],
            key_block[:, :key_count],
            value_block[:, :key_count],
            allowed,
            HD,
        )
        results.append(result)
        query_grads.append(grad_query.astype(jnp.bfloat16))
        grad_key = grad_key.at[:, :key_count].add(part_key)
        grad_value = grad_value.at[:, :key_count].add(part_value)
    next_last_k, next_last_v = passed_along(
        (grad_key[0, :halo_len], grad_value[0, :halo_len]), "seq", -1
    )
    next_k = jnp.concatenate([grad_key[1:, :halo_len], next_last_k[None]], axis=0)
    next_v = jnp.concatenate([grad_value[1:, :halo_len], next_last_v[None]], axis=0)
    own_k = jnp.concatenate(
        [grad_key[:, halo_len : halo_len + rest_len], grad_key[:, halo_len + rest_len :] + next_k],
        axis=1,
    ).reshape(group_rows, HD)
    own_v = jnp.concatenate(
        [
            grad_value[:, halo_len : halo_len + rest_len],
            grad_value[:, halo_len + rest_len :] + next_v,
        ],
        axis=1,
    ).reshape(group_rows, HD)
    all_results = jnp.concatenate(results, axis=1).reshape(group_rows, HD)
    all_query_grads = jnp.concatenate(query_grads, axis=1).reshape(group_rows, HD)
    outputs, query_grad = (
        lax.all_to_all(all_results, "head", split_axis=0, concat_axis=1, tiled=True),
        lax.all_to_all(all_query_grads, "head", split_axis=0, concat_axis=1, tiled=True),
    )
    wide_gk, wide_gv = (
        lax.all_to_all(own_k, "head", split_axis=0, concat_axis=1, tiled=True),
        lax.all_to_all(own_v, "head", split_axis=0, concat_axis=1, tiled=True),
    )
    group_total = wide_gk.shape[1] // (GROUP * HD)
    key_grad = (
        wide_gk.reshape(tok_count, group_total, GROUP, HD)
        .sum(axis=2)
        .reshape(tok_count, group_total * HD)
        .astype(jnp.bfloat16)
    )
    value_grad = (
        wide_gv.reshape(tok_count, group_total, GROUP, HD)
        .sum(axis=2)
        .reshape(tok_count, group_total * HD)
        .astype(jnp.bfloat16)
    )
    return (outputs, query_grad, key_grad, value_grad)


def solution(mesh):
    placed = (
        P(("seq", "head"), None),
        P(("seq", "head"), None),
        P(("seq", "head"), None),
        P(("seq", "head"), None),
        P(),
    )
    return jax.shard_map(
        per_device,
        mesh=mesh,
        in_specs=placed,
        out_specs=(
            P(("seq", "head"), None),
            P(("seq", "head"), None),
            P(("seq", "head"), None),
            P(("seq", "head"), None),
        ),
        check_vma=False,
    )
```

profile of v0, /device:TPU:8, one launch (start us, length us, event | category | flops | bytes accessed | tf_op | source)
XLA Modules:
  0.0 94.2 jit_solution(2533710951645964501)
XLA Ops:
  0.6 0.0 copy-start.2
  0.6 6.1 %all_gather.7 = bf16[1024,128]{1,0:T(8,128)(2,1)S(1)} all-gather(bf16[256,128]{1,0:T(8,128)(2,1)} %param.19), channel_id=1, replica_groups=mesh['seq'=8,'head'=4] {'head'}, dimensions={0}, use_global_device_ids=true | all-gather | bytes 327680 | tf_op jit(solution)/shard_map/all_gather | solution.py:80
  6.8 3.5 %collective-permute-start.1 = (bf16[64,128]{1,0:T(8,128)(2,1)S(1)}, bf16[64,128]{1,0:T(8,128)(2,1)S(1)}, u32[]{:S(2)}, u32[]{:S(2)}) collective-permute-start(bf16[64,128]{1,0:T(8,128)(2,1)S(1)} %slice_bitcast_fusion.2), channel_id=1, source_target_pairs={{0,4},{4,8},{8,12},{12,16},{16,20},{20,24},{24,28},{1,5},{5,9},{9,... | collective-permute-start | bytes 49160 | tf_op jit(solution)/shard_map/ppermute | solution.py:16
  10.3 0.0 copy-done.2
  10.3 5.8 %all_gather.6 = bf16[1024,128]{1,0:T(8,128)(2,1)S(1)} all-gather(bf16[256,128]{1,0:T(8,128)(2,1)S(1)} %copy-done.2), channel_id=1, replica_groups=mesh['seq'=8,'head'=4] {'head'}, dimensions={0}, use_global_device_ids=true | all-gather | bytes 327680 | tf_op jit(solution)/shard_map/all_gather | solution.py:79
  16.1 3.4 %collective-permute-start = (bf16[64,128]{1,0:T(8,128)(2,1)S(1)}, bf16[64,128]{1,0:T(8,128)(2,1)S(1)}, u32[]{:S(2)}, u32[]{:S(2)}) collective-permute-start(bf16[64,128]{1,0:T(8,128)(2,1)S(1)} %slice_bitcast_fusion.3), channel_id=1, source_target_pairs={{0,4},{4,8},{8,12},{12,16},{16,20},{20,24},{24,28},{1,5},{5,9},{9,... | collective-permute-start | bytes 49160 | tf_op jit(solution)/shard_map/ppermute | solution.py:16
  19.6 0.0 copy-done
  19.6 0.1 copy.12
  19.7 0.8 copy.13
  20.6 3.5 %all-to-all-start.2 = ((bf16[256,4,128]{2,0,1:T(8,128)(2,1)}), bf16[256,4,128]{2,0,1:T(8,128)(2,1)S(1)}, u32[]{:S(2)}, u32[]{:S(2)}) async-start(bf16[256,4,128]{2,0,1:T(8,128)(2,1)} %copy.13), calls=%async_computation.2 | async-start | bytes 524288 | tf_op jit(solution)/shard_map/all_to_all | solution.py:76
  24.1 0.0 copy-start.1
  24.1 0.0 copy-start.11
  24.2 0.0 copy-start.9
  24.2 0.1 dynamic_slice.8
  24.3 0.6 dynamic_slice.9
  24.9 0.1 iota_compare_fusion.1
  25.0 0.1 broadcast_compare_fusion
  25.1 0.0 copy-start.5
  25.1 0.7 add_add_fusion
  25.9 0.0 copy-start.3
  25.9 0.1 copy.9
  26.0 0.8 copy.10
  26.9 3.2 %all-to-all-done.2 = bf16[256,4,128]{2,0,1:T(8,128)(2,1)S(1)} async-done(((bf16[256,4,128]{2,0,1:T(8,128)(2,1)}), bf16[256,4,128]{2,0,1:T(8,128)(2,1)S(1)}, u32[]{:S(2)}, u32[]{:S(2)}) %all-to-all-start.2) | async-done | bytes 262176 | tf_op jit(solution)/shard_map/all_to_all | solution.py:76
  30.1 3.4 %all-to-all-start = ((bf16[256,4,128]{2,0,1:T(8,128)(2,1)}), bf16[256,4,128]{2,0,1:T(8,128)(2,1)S(1)}, u32[]{:S(2)}, u32[]{:S(2)}) async-start(bf16[256,4,128]{2,0,1:T(8,128)(2,1)} %copy.10), calls=%async_computation | async-start | bytes 524288 | tf_op jit(solution)/shard_map/all_to_all | solution.py:75
  33.5 0.0 collective-permute-done.1
  33.5 0.2 convolution_bitcast_fusion
  33.8 0.2 convolution_bitcast_fusion.1
  34.0 0.0 collective-permute-done
  34.0 0.0 copy-start.6
  34.0 5.5 %all-to-all-done = bf16[256,4,128]{2,0,1:T(8,128)(2,1)S(1)} async-done(((bf16[256,4,128]{2,0,1:T(8,128)(2,1)}), bf16[256,4,128]{2,0,1:T(8,128)(2,1)S(1)}, u32[]{:S(2)}, u32[]{:S(2)}) %all-to-all-start) | async-done | bytes 262176 | tf_op jit(solution)/shard_map/all_to_all | solution.py:75
  39.5 0.5 fusion.106
  40.0 0.7 convolution_convert_fusion.3
  40.7 1.3 %fusion.43 = f32[4,192,128]{2,1,0:T(8,128)} fusion(bf16[4,256,128]{2,1,0:T(8,128)(2,1)S(1)} %bitcast.71, f32[4,128]{1,0:T(4,128)S(1)} %get-tuple-element.74, bf16[4,256,128]{2,1,0:T(8,128)(2,1)S(1)} %bitcast.91, bf16[4,256,128]{2,1,0:T(8,128)(2,1)S(1)} %bitcast.83, bf16[3,64,128]{2,1,0:T(8,128)(2,1)S(1)} %slice.163, bf16[1,64,128]{2,1,0:T(8,128)(2,1)S(1)} %bitcast.105, ...), kind=kOutput, calls=%fused_computation.65 | convolution fusion | flops 53084864 | bytes 1040384 | tf_op jit(solution)/shard_map/dot_general | solution.py:60
  42.0 1.5 %fusion.103 = (f32[4,128]{1,0:T(4,128)S(1)}, f32[4,128,320]{1,2,0:T(8,128)}) fusion(bf16[4,256,128]{2,1,0:T(8,128)(2,1)S(1)} %bitcast.84, bf16[3,64,128]{2,1,0:T(8,128)(2,1)S(1)} %slice.163, bf16[1,64,128]{2,1,0:T(8,128)(2,1)S(1)} %bitcast.106, bf16[4,256,128]{2,1,0:T(8,128)(2,1)S(1)} %bitcast.92, pred[4]{0:T(512)(128)(4,1)S(1)} %add_compare_fusion, ...), kind=kOutput, calls=%fused_computation.111 | convolution fusion | flops 46367040 | bytes 1207296 | tf_op jit(solution)/shard_map/sub | solution.py:43
  43.6 0.0 copy-done.5
  43.6 0.9 %convolution_convert_fusion.2 = bf16[4,128,128]{2,1,0:T(8,128)(2,1)S(1)} fusion(bf16[4,256,128]{2,1,0:T(8,128)(2,1)S(1)} %bitcast.68, bf16[3,64,128]{2,1,0:T(8,128)(2,1)S(1)} %slice.166, bf16[1,64,128]{2,1,0:T(8,128)(2,1)S(1)} %bitcast.100, f32[4,128]{1,0:T(4,128)S(1)} %get-tuple-element.72, bf16[4,256,128]{2,1,0:T(8,128)(2,1)S(1)} %bitcast.85, ...), kind=kOutput, calls=%fused_computation.30 | convolution fusion | flops 89523008 | bytes 1010688 | tf_op jit(solution)/shard_map/dot_general | solution.py:46
  44.5 0.7 pad_maximum_fusion.4
  45.3 3.4 %all-to-all-start.1 = ((bf16[4,256,128]{2,1,0:T(8,128)(2,1)}), bf16[4,256,128]{2,1,0:T(8,128)(2,1)S(1)}, u32[]{:S(2)}, u32[]{:S(2)}) async-start(bf16[4,256,128]{2,1,0:T(8,128)(2,1)} %pad_maximum_fusion.4), calls=%async_computation.1 | async-start | bytes 524288 | tf_op jit(solution)/shard_map/all_to_all | solution.py:147
  48.7 1.7 %convolution_convert_fusion = bf16[4,128,128]{2,1,0:T(8,128)(2,1)S(1)} fusion(f32[4,128,320]{1,2,0:T(8,128)S(1)} %convolution_bitcast_fusion, bf16[4,256,128]{2,1,0:T(8,128)(2,1)S(1)} %bitcast.86, bf16[3,64,128]{2,1,0:T(8,128)(2,1)S(1)} %slice.163, bf16[1,64,128]{2,1,0:T(8,128)(2,1)S(1)} %bitcast.108, f32[4,128,320]{1,2,0:T(8,128)} %get-tuple-element.73, ...), kind=kOutput, calls=%fused_computation.28 | convolution fusion | flops 44139328 | bytes 1771520 | tf_op jit(solution)/shard_map/dot_general | solution.py:54
  50.4 1.0 %fusion.22 = f32[4,192,128]{2,1,0:T(8,128)} fusion(f32[4,128,192]{1,2,0:T(8,128)S(1)} %convolution_bitcast_fusion.1, bf16[4,256,128]{2,1,0:T(8,128)(2,1)S(1)} %bitcast.94, f32[4,128,192]{1,2,0:T(8,128)S(1)} %get-tuple-element.75, f32[4,128]{1,0:T(4,128)S(1)} %get-tuple-element.74), kind=kOutput, calls=%fused_computation.32 | convolution fusion | flops 25854656 | bytes 2101248 | tf_op jit(solution)/shard_map/dot_general | solution.py:57
  51.4 1.7 %convolution_add_fusion.1 = f32[4,320,128]{2,1,0:T(8,128)S(1)} fusion(f32[4,128,320]{1,2,0:T(8,128)S(1)} %convolution_bitcast_fusion, f32[4,192,128]{2,1,0:T(8,128)} %fusion.22, bf16[4,256,128]{2,1,0:T(8,128)(2,1)S(1)} %bitcast.95, f32[4,128,320]{1,2,0:T(8,128)} %get-tuple-element.73, f32[4,128]{1,0:T(4,128)S(1)} %get-tuple-element.72), kind=kOutput, calls=%fused_computation.11 | convolution fusion | flops 43254592 | bytes 3805184 | tf_op jit(solution)/shard_map/dot_general | solution.py:57
  53.2 0.0 copy-start.7
  53.2 3.3 %collective-permute-start.2 = (f32[64,128]{1,0:T(8,128)S(1)}, f32[64,128]{1,0:T(8,128)S(1)}, u32[]{:S(2)}, u32[]{:S(2)}) collective-permute-start(f32[64,128]{1,0:T(8,128)S(1)} %slice_bitcast_fusion.1), channel_id=1, source_target_pairs={{4,0},{8,4},{12,8},{16,12},{20,16},{24,20},{28,24},{5,1},{9,5},{13... | collective-permute-start | bytes 98312 | tf_op jit(solution)/shard_map/ppermute | solution.py:16
  56.6 1.9 %convolution_add_fusion = f32[4,320,128]{2,1,0:T(8,128)S(1)} fusion(f32[4,192,128]{2,1,0:T(8,128)} %fusion.43, bf16[4,256,128]{2,1,0:T(8,128)(2,1)S(1)} %bitcast.72, f32[4,128]{1,0:T(4,128)S(1)} %get-tuple-element.72, bf16[4,256,128]{2,1,0:T(8,128)(2,1)S(1)} %bitcast.87, bf16[3,64,128]{2,1,0:T(8,128)(2,1)S(1)} %copy-done.4, ...), kind=kOutput, calls=%fused_computation.10 | convolution fusion | flops 88638272 | bytes 1731584 | tf_op jit(solution)/shard_map/dot_general | solution.py:60
  58.4 0.4 convolution_convert_fusion.1
  58.8 0.7 pad_maximum_fusion.5
  59.6 0.0 all-to-all-done.1
  59.6 3.4 %all-to-all-start.3 = ((bf16[4,256,128]{2,1,0:T(8,128)(2,1)}), bf16[4,256,128]{2,1,0:T(8,128)(2,1)S(1)}, u32[]{:S(2)}, u32[]{:S(2)}) async-start(bf16[4,256,128]{2,1,0:T(8,128)(2,1)} %pad_maximum_fusion.5), calls=%async_computation.3 | async-start | bytes 524288 | tf_op jit(solution)/shard_map/all_to_all | solution.py:148
  63.0 0.0 collective-permute-done.2
  63.0 0.8 pad_maximum_fusion
  63.9 5.1 %all-to-all-done.3 = bf16[4,256,128]{2,1,0:T(8,128)(2,1)S(1)} async-done(((bf16[4,256,128]{2,1,0:T(8,128)(2,1)}), bf16[4,256,128]{2,1,0:T(8,128)(2,1)S(1)}, u32[]{:S(2)}, u32[]{:S(2)}) %all-to-all-start.3) | async-done | bytes 262176 | tf_op jit(solution)/shard_map/all_to_all | solution.py:148
  69.0 3.5 %all-to-all-start.4 = ((f32[4,256,128]{2,1,0:T(8,128)}), f32[4,256,128]{2,1,0:T(8,128)S(1)}, u32[]{:S(2)}, u32[]{:S(2)}) async-start(f32[4,256,128]{2,1,0:T(8,128)} %pad_maximum_fusion), calls=%async_computation.4 | async-start | bytes 1048576 | tf_op jit(solution)/shard_map/all_to_all | solution.py:151
  72.5 2.4 %collective-permute-start.3 = (f32[64,128]{1,0:T(8,128)S(1)}, f32[64,128]{1,0:T(8,128)S(1)}, u32[]{:S(2)}, u32[]{:S(2)}) collective-permute-start(f32[64,128]{1,0:T(8,128)S(1)} %slice_bitcast_fusion), channel_id=1, source_target_pairs={{4,0},{8,4},{12,8},{16,12},{20,16},{24,20},{28,24},{5,1},{9,5},{13... | collective-permute-start | bytes 98312 | tf_op jit(solution)/shard_map/ppermute | solution.py:16
  75.0 3.3 %collective-permute-done.3 = f32[64,128]{1,0:T(8,128)S(1)} collective-permute-done((f32[64,128]{1,0:T(8,128)S(1)}, f32[64,128]{1,0:T(8,128)S(1)}, u32[]{:S(2)}, u32[]{:S(2)}) %collective-permute-start.3) | collective-permute-done | bytes 32800 | tf_op jit(solution)/shard_map/ppermute | solution.py:16
  78.3 0.8 pad_maximum_fusion.1
  79.2 2.1 %all-to-all-done.4 = f32[4,256,128]{2,1,0:T(8,128)S(1)} async-done(((f32[4,256,128]{2,1,0:T(8,128)}), f32[4,256,128]{2,1,0:T(8,128)S(1)}, u32[]{:S(2)}, u32[]{:S(2)}) %all-to-all-start.4) | async-done | bytes 524320 | tf_op jit(solution)/shard_map/all_to_all | solution.py:151
  81.3 3.5 %all-to-all-start.5 = ((f32[4,256,128]{2,1,0:T(8,128)}), f32[4,256,128]{2,1,0:T(8,128)S(1)}, u32[]{:S(2)}, u32[]{:S(2)}) async-start(f32[4,256,128]{2,1,0:T(8,128)} %pad_maximum_fusion.1), calls=%async_computation.5 | async-start | bytes 1048576 | tf_op jit(solution)/shard_map/all_to_all | solution.py:152
  84.8 0.1 copy.11
  84.9 0.8 copy.15
  85.8 0.1 copy.14
  85.9 0.8 copy.16
  86.8 0.7 reduce_sum.58
  87.4 6.2 %all-to-all-done.5 = f32[4,256,128]{2,1,0:T(8,128)S(1)} async-done(((f32[4,256,128]{2,1,0:T(8,128)}), f32[4,256,128]{2,1,0:T(8,128)S(1)}, u32[]{:S(2)}, u32[]{:S(2)}) %all-to-all-start.5) | async-done | bytes 524320 | tf_op jit(solution)/shard_map/all_to_all | solution.py:152
  93.6 0.7 reduce_sum.59
  (33 shorter events, 0.2 us)
Async XLA Ops:
  0.6 9.7 %copy-start.2 = (bf16[256,128]{1,0:T(8,128)(2,1)S(1)}, bf16[256,128]{1,0:T(8,128)(2,1)}, u32[]{:S(2)}) copy-start(bf16[256,128]{1,0:T(8,128)(2,1)} %param.18) | copy-start | bytes 196612
  6.8 12.8 %copy-start = (bf16[256,512]{1,0:T(8,128)(2,1)S(1)}, bf16[256,512]{1,0:T(8,128)(2,1)}, u32[]{:S(2)}) copy-start(bf16[256,512]{1,0:T(8,128)(2,1)} %param.20) | copy-start | bytes 786436
  6.8 26.7 %collective-permute-start.1 = (bf16[64,128]{1,0:T(8,128)(2,1)S(1)}, bf16[64,128]{1,0:T(8,128)(2,1)S(1)}, u32[]{:S(2)}, u32[]{:S(2)}) collective-permute-start(bf16[64,128]{1,0:T(8,128)(2,1)S(1)} %slice_bitcast_fusion.2), channel_id=1, source_target_pairs={{0,4},{4,8},{8,12},{12,16},{16,20},{20,24},{24,28},{1,5},{5,9},{9,... | collective-permute-start | bytes 49160 | tf_op jit(solution)/shard_map/ppermute | solution.py:16
  16.1 17.9 %collective-permute-start = (bf16[64,128]{1,0:T(8,128)(2,1)S(1)}, bf16[64,128]{1,0:T(8,128)(2,1)S(1)}, u32[]{:S(2)}, u32[]{:S(2)}) collective-permute-start(bf16[64,128]{1,0:T(8,128)(2,1)S(1)} %slice_bitcast_fusion.3), channel_id=1, source_target_pairs={{0,4},{4,8},{8,12},{12,16},{16,20},{20,24},{24,28},{1,5},{5,9},{9,... | collective-permute-start | bytes 49160 | tf_op jit(solution)/shard_map/ppermute | solution.py:16
  20.5 3.7 %copy-start.8 = (s32[32]{0:T(128)S(1)}, s32[32]{0:T(128)}, u32[]{:S(2)}) copy-start(s32[32]{0:T(128)} %param.21) | copy-start | bytes 388
  20.6 9.5 %all-to-all-start.2 = ((bf16[256,4,128]{2,0,1:T(8,128)(2,1)}), bf16[256,4,128]{2,0,1:T(8,128)(2,1)S(1)}, u32[]{:S(2)}, u32[]{:S(2)}) async-start(bf16[256,4,128]{2,0,1:T(8,128)(2,1)} %copy.13), calls=%async_computation.2 | async-start | bytes 524288 | tf_op jit(solution)/shard_map/all_to_all | solution.py:76
  24.1 1.8 %copy-start.1 = (bf16[256,512]{1,0:T(8,128)(2,1)S(1)}, bf16[256,512]{1,0:T(8,128)(2,1)}, u32[]{:S(2)}) copy-start(bf16[256,512]{1,0:T(8,128)(2,1)} %param.17) | copy-start | bytes 786436
  24.1 19.4 %copy-start.11 = (pred[320]{0:T(512)(128)(4,1)}, pred[320]{0:T(512)(128)(4,1)S(1)}, u32[]{:S(2)}) copy-start(pred[320]{0:T(512)(128)(4,1)S(1)} %broadcast_compare_fusion.1) | copy-start | bytes 964
  24.2 19.4 %copy-start.9 = (pred[4]{0:T(512)(128)(4,1)}, pred[4]{0:T(512)(128)(4,1)S(1)}, u32[]{:S(2)}) copy-start(pred[4]{0:T(512)(128)(4,1)S(1)} %add_compare_fusion) | copy-start | bytes 16
  25.1 18.5 %copy-start.5 = (pred[128,320]{0,1:T(8,128)(4,1)}, pred[128,320]{0,1:T(8,128)(4,1)S(1)}, u32[]{:S(2)}) copy-start(pred[128,320]{0,1:T(8,128)(4,1)S(1)} %broadcast_compare_fusion) | copy-start | bytes 122884
  25.9 22.8 %copy-start.3 = (bf16[3,64,128]{2,1,0:T(8,128)(2,1)}, bf16[3,64,128]{2,1,0:T(8,128)(2,1)S(1)}, u32[]{:S(2)}) copy-start(bf16[3,64,128]{2,1,0:T(8,128)(2,1)S(1)} %slice.163) | copy-start | bytes 147460
  30.1 9.4 %all-to-all-start = ((bf16[256,4,128]{2,0,1:T(8,128)(2,1)}), bf16[256,4,128]{2,0,1:T(8,128)(2,1)S(1)}, u32[]{:S(2)}, u32[]{:S(2)}) async-start(bf16[256,4,128]{2,0,1:T(8,128)(2,1)} %copy.10), calls=%async_computation | async-start | bytes 524288 | tf_op jit(solution)/shard_map/all_to_all | solution.py:75
  34.0 14.7 %copy-start.6 = (bf16[64,128]{1,0:T(8,128)(2,1)}, bf16[64,128]{1,0:T(8,128)(2,1)S(1)}, u32[]{:S(2)}) copy-start(bf16[64,128]{1,0:T(8,128)(2,1)S(1)} %collective-permute-done) | copy-start | bytes 49156
  45.3 14.3 %all-to-all-start.1 = ((bf16[4,256,128]{2,1,0:T(8,128)(2,1)}), bf16[4,256,128]{2,1,0:T(8,128)(2,1)S(1)}, u32[]{:S(2)}, u32[]{:S(2)}) async-start(bf16[4,256,128]{2,1,0:T(8,128)(2,1)} %pad_maximum_fusion.4), calls=%async_computation.1 | async-start | bytes 524288 | tf_op jit(solution)/shard_map/all_to_all | solution.py:147
  51.4 5.1 %copy-start.10 = (pred[4]{0:T(512)(128)(4,1)S(1)}, pred[4]{0:T(512)(128)(4,1)}, u32[]{:S(2)}) copy-start(pred[4]{0:T(512)(128)(4,1)} %copy-done.9) | copy-start | bytes 16
  51.4 5.1 %copy-start.12 = (pred[320]{0:T(512)(128)(4,1)S(1)}, pred[320]{0:T(512)(128)(4,1)}, u32[]{:S(2)}) copy-start(pred[320]{0:T(512)(128)(4,1)} %copy-done.11) | copy-start | bytes 964
  53.2 3.4 %copy-start.4 = (bf16[3,64,128]{2,1,0:T(8,128)(2,1)S(1)}, bf16[3,64,128]{2,1,0:T(8,128)(2,1)}, u32[]{:S(2)}) copy-start(bf16[3,64,128]{2,1,0:T(8,128)(2,1)} %copy-done.3) | copy-start | bytes 147460
  53.2 3.4 %copy-start.7 = (bf16[64,128]{1,0:T(8,128)(2,1)S(1)}, bf16[64,128]{1,0:T(8,128)(2,1)}, u32[]{:S(2)}) copy-start(bf16[64,128]{1,0:T(8,128)(2,1)} %copy-done.6) | copy-start | bytes 49156
  53.2 9.8 %collective-permute-start.2 = (f32[64,128]{1,0:T(8,128)S(1)}, f32[64,128]{1,0:T(8,128)S(1)}, u32[]{:S(2)}, u32[]{:S(2)}) collective-permute-start(f32[64,128]{1,0:T(8,128)S(1)} %slice_bitcast_fusion.1), channel_id=1, source_target_pairs={{4,0},{8,4},{12,8},{16,12},{20,16},{24,20},{28,24},{5,1},{9,5},{13... | collective-permute-start | bytes 98312 | tf_op jit(solution)/shard_map/ppermute | solution.py:16
  59.6 9.4 %all-to-all-start.3 = ((bf16[4,256,128]{2,1,0:T(8,128)(2,1)}), bf16[4,256,128]{2,1,0:T(8,128)(2,1)S(1)}, u32[]{:S(2)}, u32[]{:S(2)}) async-start(bf16[4,256,128]{2,1,0:T(8,128)(2,1)} %pad_maximum_fusion.5), calls=%async_computation.3 | async-start | bytes 524288 | tf_op jit(solution)/shard_map/all_to_all | solution.py:148
  69.0 12.3 %all-to-all-start.4 = ((f32[4,256,128]{2,1,0:T(8,128)}), f32[4,256,128]{2,1,0:T(8,128)S(1)}, u32[]{:S(2)}, u32[]{:S(2)}) async-start(f32[4,256,128]{2,1,0:T(8,128)} %pad_maximum_fusion), calls=%async_computation.4 | async-start | bytes 1048576 | tf_op jit(solution)/shard_map/all_to_all | solution.py:151
  72.5 5.8 %collective-permute-start.3 = (f32[64,128]{1,0:T(8,128)S(1)}, f32[64,128]{1,0:T(8,128)S(1)}, u32[]{:S(2)}, u32[]{:S(2)}) collective-permute-start(f32[64,128]{1,0:T(8,128)S(1)} %slice_bitcast_fusion), channel_id=1, source_target_pairs={{4,0},{8,4},{12,8},{16,12},{20,16},{24,20},{28,24},{5,1},{9,5},{13... | collective-permute-start | bytes 98312 | tf_op jit(solution)/shard_map/ppermute | solution.py:16
  81.3 12.3 %all-to-all-start.5 = ((f32[4,256,128]{2,1,0:T(8,128)}), f32[4,256,128]{2,1,0:T(8,128)S(1)}, u32[]{:S(2)}, u32[]{:S(2)}) async-start(f32[4,256,128]{2,1,0:T(8,128)} %pad_maximum_fusion.1), calls=%async_computation.5 | async-start | bytes 1048576 | tf_op jit(solution)/shard_map/all_to_all | solution.py:152
where the time goes:
time: 95.1 us; the launch traced here: 94.2 us
  starting transfers between devices  33.4 us (35%)
  waiting for transfers between devices  25.5 us (27%)
  matrix products  12.1 us (13%)
  blocking collectives  11.9 us (13%)
  other arithmetic  5.42 us (6%)
  local copies, waits for them, and re-layouts  4.74 us (5%)
  between operations  1.09 us (1%)
    ppermute x4, starting transfers between devices, passed_along(): lax.ppermute(value, axis, [(source, source + steps) for source in range(f...  12.7 us
    all_to_all x1, waiting for transfers between devices, per_device(): lax.all_to_all(own_v, 'head', split_axis=0, concat_axis=1, tiled=True)  6.16 us
    all_gather x1, blocking collectives, per_device(): lax.all_gather(value_rows, 'head', axis=0, tiled=True)  6.13 us
    all_gather x1, blocking collectives, per_device(): lax.all_gather(key_rows, 'head', axis=0, tiled=True)  5.79 us
    all_to_all x1, waiting for transfers between devices, per_device(): lax.all_to_all(queries, 'head', split_axis=1, concat_axis=0, tiled=True)  5.5 us
    all_to_all x1, waiting for transfers between devices, per_device(): lax.all_to_all(all_query_grads, 'head', split_axis=0, concat_axis=1, tile...  5.14 us
    all_to_all x1, starting transfers between devices, per_device(): lax.all_to_all(out_grad, 'head', split_axis=1, concat_axis=0, tiled=True)  3.54 us
    all_to_all x1, starting transfers between devices, per_device(): lax.all_to_all(own_v, 'head', split_axis=0, concat_axis=1, tiled=True)  3.47 us
  transfers between devices with their start and end apart: 10, of which 6 were waited for; matrix products, arithmetic and copies ran while one was open for 17% of the time, Pallas kernels for 0%

commit v1 on v0

--- a/solution.py
+++ b/solution.py
@@ -144,7 +144,12 @@
     all_results = jnp.concatenate(results, axis=1).reshape(group_rows, HD)
     all_query_grads = jnp.concatenate(query_grads, axis=1).reshape(group_rows, HD)
     outputs, query_grad = (
-        lax.all_to_all(all_results, "head", split_axis=0, concat_axis=1, tiled=True),
+        jnp.concatenate(
+            lax.all_to_all(
+                jnp.stack(jnp.split(all_results, lax.axis_size("head"), axis=0)), "head", 0, 0
+            ),
+            axis=1,
+        ),
         lax.all_to_all(all_query_grads, "head", split_axis=0, concat_axis=1, tiled=True),
     )
     wide_gk, wide_gv = (

time: 95.1 us -> 95.1 us (level)
  no operation moved by 1% of the time
where the time goes in v1:
time: 95.1 us; the launch traced here: 94.2 us
  starting transfers between devices  33.4 us (35%)
  waiting for transfers between devices  25.5 us (27%)
  matrix products  12.1 us (13%)
  blocking collectives  11.9 us (13%)
  other arithmetic  5.42 us (6%)
  local copies, waits for them, and re-layouts  4.74 us (5%)
  between operations  1.09 us (1%)
    ppermute x4, starting transfers between devices, passed_along(): lax.ppermute(value, axis, [(source, source + steps) for source in range(f...  12.7 us
    all_to_all x1, waiting for transfers between devices, per_device(): lax.all_to_all(own_v, 'head', split_axis=0, concat_axis=1, tiled=True)  6.16 us
    all_gather x1, blocking collectives, per_device(): lax.all_gather(value_rows, 'head', axis=0, tiled=True)  6.13 us
    all_gather x1, blocking collectives, per_device(): lax.all_gather(key_rows, 'head', axis=0, tiled=True)  5.79 us
    all_to_all x1, waiting for transfers between devices, per_device(): lax.all_to_all(queries, 'head', split_axis=1, concat_axis=0, tiled=True)  5.5 us
    all_to_all x1, waiting for transfers between devices, per_device(): lax.all_to_all(all_query_grads, 'head', split_axis=0, concat_axis=1, tile...  5.14 us
    all_to_all x1, starting transfers between devices, per_device(): lax.all_to_all(out_grad, 'head', split_axis=1, concat_axis=0, tiled=True)  3.54 us
    all_to_all x1, starting transfers between devices, per_device(): lax.all_to_all(own_v, 'head', split_axis=0, concat_axis=1, tiled=True)  3.47 us
  transfers between devices with their start and end apart: 10, of which 6 were waited for; matrix products, arithmetic and copies ran while one was open for 17% of the time, Pallas kernels for 0%

profile of v1, /device:TPU:8, one launch (start us, length us, event | category | flops | bytes accessed | tf_op | source)
XLA Modules:
  0.0 94.2 jit_solution(2533710951645964501)
XLA Ops:
  0.6 0.0 copy-start.2
  0.6 6.1 %all_gather.7 = bf16[1024,128]{1,0:T(8,128)(2,1)S(1)} all-gather(bf16[256,128]{1,0:T(8,128)(2,1)} %param.19), channel_id=1, replica_groups=mesh['seq'=8,'head'=4] {'head'}, dimensions={0}, use_global_device_ids=true | all-gather | bytes 327680 | tf_op jit(solution)/shard_map/all_gather | solution.py:80
  6.8 3.5 %collective-permute-start.1 = (bf16[64,128]{1,0:T(8,128)(2,1)S(1)}, bf16[64,128]{1,0:T(8,128)(2,1)S(1)}, u32[]{:S(2)}, u32[]{:S(2)}) collective-permute-start(bf16[64,128]{1,0:T(8,128)(2,1)S(1)} %slice_bitcast_fusion.2), channel_id=1, source_target_pairs={{0,4},{4,8},{8,12},{12,16},{16,20},{20,24},{24,28},{1,5},{5,9},{9,... | collective-permute-start | bytes 49160 | tf_op jit(solution)/shard_map/ppermute | solution.py:16
  10.3 0.0 copy-done.2
  10.3 5.8 %all_gather.6 = bf16[1024,128]{1,0:T(8,128)(2,1)S(1)} all-gather(bf16[256,128]{1,0:T(8,128)(2,1)S(1)} %copy-done.2), channel_id=1, replica_groups=mesh['seq'=8,'head'=4] {'head'}, dimensions={0}, use_global_device_ids=true | all-gather | bytes 327680 | tf_op jit(solution)/shard_map/all_gather | solution.py:79
  16.1 3.4 %collective-permute-start = (bf16[64,128]{1,0:T(8,128)(2,1)S(1)}, bf16[64,128]{1,0:T(8,128)(2,1)S(1)}, u32[]{:S(2)}, u32[]{:S(2)}) collective-permute-start(bf16[64,128]{1,0:T(8,128)(2,1)S(1)} %slice_bitcast_fusion.3), channel_id=1, source_target_pairs={{0,4},{4,8},{8,12},{12,16},{16,20},{20,24},{24,28},{1,5},{5,9},{9,... | collective-permute-start | bytes 49160 | tf_op jit(solution)/shard_map/ppermute | solution.py:16
  19.6 0.0 copy-done
  19.6 0.1 copy.12
  19.7 0.8 copy.13
  20.6 3.5 %all-to-all-start.2 = ((bf16[256,4,128]{2,0,1:T(8,128)(2,1)}), bf16[256,4,128]{2,0,1:T(8,128)(2,1)S(1)}, u32[]{:S(2)}, u32[]{:S(2)}) async-start(bf16[256,4,128]{2,0,1:T(8,128)(2,1)} %copy.13), calls=%async_computation.2 | async-start | bytes 524288 | tf_op jit(solution)/shard_map/all_to_all | solution.py:76
  24.1 0.0 copy-start.1
  24.1 0.0 copy-start.11
  24.2 0.0 copy-start.9
  24.2 0.1 dynamic_slice.8
  24.3 0.6 dynamic_slice.9
  24.9 0.1 iota_compare_fusion.1
  25.0 0.1 broadcast_compare_fusion
  25.1 0.0 copy-start.5
  25.1 0.7 add_add_fusion
  25.9 0.0 copy-start.3
  25.9 0.1 copy.9
  26.0 0.8 copy.10
  26.9 3.2 %all-to-all-done.2 = bf16[256,4,128]{2,0,1:T(8,128)(2,1)S(1)} async-done(((bf16[256,4,128]{2,0,1:T(8,128)(2,1)}), bf16[256,4,128]{2,0,1:T(8,128)(2,1)S(1)}, u32[]{:S(2)}, u32[]{:S(2)}) %all-to-all-start.2) | async-done | bytes 262176 | tf_op jit(solution)/shard_map/all_to_all | solution.py:76
  30.1 3.4 %all-to-all-start = ((bf16[256,4,128]{2,0,1:T(8,128)(2,1)}), bf16[256,4,128]{2,0,1:T(8,128)(2,1)S(1)}, u32[]{:S(2)}, u32[]{:S(2)}) async-start(bf16[256,4,128]{2,0,1:T(8,128)(2,1)} %copy.10), calls=%async_computation | async-start | bytes 524288 | tf_op jit(solution)/shard_map/all_to_all | solution.py:75
  33.5 0.0 collective-permute-done.1
  33.5 0.2 convolution_bitcast_fusion
  33.8 0.2 convolution_bitcast_fusion.1
  34.0 0.0 collective-permute-done
  34.0 0.0 copy-start.6
  34.0 5.5 %all-to-all-done = bf16[256,4,128]{2,0,1:T(8,128)(2,1)S(1)} async-done(((bf16[256,4,128]{2,0,1:T(8,128)(2,1)}), bf16[256,4,128]{2,0,1:T(8,128)(2,1)S(1)}, u32[]{:S(2)}, u32[]{:S(2)}) %all-to-all-start) | async-done | bytes 262176 | tf_op jit(solution)/shard_map/all_to_all | solution.py:75
  39.5 0.5 fusion.106
  40.0 0.7 convolution_convert_fusion.3
  40.7 1.3 %fusion.43 = f32[4,192,128]{2,1,0:T(8,128)} fusion(bf16[4,256,128]{2,1,0:T(8,128)(2,1)S(1)} %bitcast.71, f32[4,128]{1,0:T(4,128)S(1)} %get-tuple-element.74, bf16[4,256,128]{2,1,0:T(8,128)(2,1)S(1)} %bitcast.91, bf16[4,256,128]{2,1,0:T(8,128)(2,1)S(1)} %bitcast.83, bf16[3,64,128]{2,1,0:T(8,128)(2,1)S(1)} %slice.168, bf16[1,64,128]{2,1,0:T(8,128)(2,1)S(1)} %bitcast.105, ...), kind=kOutput, calls=%fused_computation.65 | convolution fusion | flops 53084864 | bytes 1040384 | tf_op jit(solution)/shard_map/dot_general | solution.py:60
  42.0 1.5 %fusion.103 = (f32[4,128]{1,0:T(4,128)S(1)}, f32[4,128,320]{1,2,0:T(8,128)}) fusion(bf16[4,256,128]{2,1,0:T(8,128)(2,1)S(1)} %bitcast.84, bf16[3,64,128]{2,1,0:T(8,128)(2,1)S(1)} %slice.168, bf16[1,64,128]{2,1,0:T(8,128)(2,1)S(1)} %bitcast.106, bf16[4,256,128]{2,1,0:T(8,128)(2,1)S(1)} %bitcast.92, pred[4]{0:T(512)(128)(4,1)S(1)} %add_compare_fusion, ...), kind=kOutput, calls=%fused_computation.111 | convolution fusion | flops 46367040 | bytes 1207296 | tf_op jit(solution)/shard_map/sub | solution.py:43
  43.6 0.0 copy-done.5
  43.6 0.9 %convolution_convert_fusion.2 = bf16[4,128,128]{2,1,0:T(8,128)(2,1)S(1)} fusion(bf16[4,256,128]{2,1,0:T(8,128)(2,1)S(1)} %bitcast.68, bf16[3,64,128]{2,1,0:T(8,128)(2,1)S(1)} %slice.171, bf16[1,64,128]{2,1,0:T(8,128)(2,1)S(1)} %bitcast.100, f32[4,128]{1,0:T(4,128)S(1)} %get-tuple-element.72, bf16[4,256,128]{2,1,0:T(8,128)(2,1)S(1)} %bitcast.85, ...), kind=kOutput, calls=%fused_computation.30 | convolution fusion | flops 89523008 | bytes 1010688 | tf_op jit(solution)/shard_map/dot_general | solution.py:46
  44.5 0.7 pad_maximum_fusion.4
  45.3 3.4 %all-to-all-start.1 = ((bf16[4,256,128]{2,1,0:T(8,128)(2,1)}), bf16[4,256,128]{2,1,0:T(8,128)(2,1)S(1)}, u32[]{:S(2)}, u32[]{:S(2)}) async-start(bf16[4,256,128]{2,1,0:T(8,128)(2,1)} %pad_maximum_fusion.4), calls=%async_computation.1 | async-start | bytes 524288 | tf_op jit(solution)/shard_map/all_to_all | solution.py:148
  48.7 1.7 %convolution_convert_fusion = bf16[4,128,128]{2,1,0:T(8,128)(2,1)S(1)} fusion(f32[4,128,320]{1,2,0:T(8,128)S(1)} %convolution_bitcast_fusion, bf16[4,256,128]{2,1,0:T(8,128)(2,1)S(1)} %bitcast.86, bf16[3,64,128]{2,1,0:T(8,128)(2,1)S(1)} %slice.168, bf16[1,64,128]{2,1,0:T(8,128)(2,1)S(1)} %bitcast.108, f32[4,128,320]{1,2,0:T(8,128)} %get-tuple-element.73, ...), kind=kOutput, calls=%fused_computation.28 | convolution fusion | flops 44139328 | bytes 1771520 | tf_op jit(solution)/shard_map/dot_general | solution.py:54
  50.4 1.0 %fusion.22 = f32[4,192,128]{2,1,0:T(8,128)} fusion(f32[4,128,192]{1,2,0:T(8,128)S(1)} %convolution_bitcast_fusion.1, bf16[4,256,128]{2,1,0:T(8,128)(2,1)S(1)} %bitcast.94, f32[4,128,192]{1,2,0:T(8,128)S(1)} %get-tuple-element.75, f32[4,128]{1,0:T(4,128)S(1)} %get-tuple-element.74), kind=kOutput, calls=%fused_computation.32 | convolution fusion | flops 25854656 | bytes 2101248 | tf_op jit(solution)/shard_map/dot_general | solution.py:57
  51.4 1.7 %convolution_add_fusion.1 = f32[4,320,128]{2,1,0:T(8,128)S(1)} fusion(f32[4,128,320]{1,2,0:T(8,128)S(1)} %convolution_bitcast_fusion, f32[4,192,128]{2,1,0:T(8,128)} %fusion.22, bf16[4,256,128]{2,1,0:T(8,128)(2,1)S(1)} %bitcast.95, f32[4,128,320]{1,2,0:T(8,128)} %get-tuple-element.73, f32[4,128]{1,0:T(4,128)S(1)} %get-tuple-element.72), kind=kOutput, calls=%fused_computation.11 | convolution fusion | flops 43254592 | bytes 3805184 | tf_op jit(solution)/shard_map/dot_general | solution.py:57
  53.2 0.0 copy-start.7
  53.2 3.3 %collective-permute-start.2 = (f32[64,128]{1,0:T(8,128)S(1)}, f32[64,128]{1,0:T(8,128)S(1)}, u32[]{:S(2)}, u32[]{:S(2)}) collective-permute-start(f32[64,128]{1,0:T(8,128)S(1)} %slice_bitcast_fusion.1), channel_id=1, source_target_pairs={{4,0},{8,4},{12,8},{16,12},{20,16},{24,20},{28,24},{5,1},{9,5},{13... | collective-permute-start | bytes 98312 | tf_op jit(solution)/shard_map/ppermute | solution.py:16
  56.6 1.9 %convolution_add_fusion = f32[4,320,128]{2,1,0:T(8,128)S(1)} fusion(f32[4,192,128]{2,1,0:T(8,128)} %fusion.43, bf16[4,256,128]{2,1,0:T(8,128)(2,1)S(1)} %bitcast.72, f32[4,128]{1,0:T(4,128)S(1)} %get-tuple-element.72, bf16[4,256,128]{2,1,0:T(8,128)(2,1)S(1)} %bitcast.87, bf16[3,64,128]{2,1,0:T(8,128)(2,1)S(1)} %copy-done.4, ...), kind=kOutput, calls=%fused_computation.10 | convolution fusion | flops 88638272 | bytes 1731584 | tf_op jit(solution)/shard_map/dot_general | solution.py:60
  58.4 0.4 convolution_convert_fusion.1
  58.8 0.7 pad_maximum_fusion.5
  59.6 0.0 all-to-all-done.1
  59.6 3.4 %all-to-all-start.3 = ((bf16[4,256,128]{2,1,0:T(8,128)(2,1)}), bf16[4,256,128]{2,1,0:T(8,128)(2,1)S(1)}, u32[]{:S(2)}, u32[]{:S(2)}) async-start(bf16[4,256,128]{2,1,0:T(8,128)(2,1)} %pad_maximum_fusion.5), calls=%async_computation.3 | async-start | bytes 524288 | tf_op jit(solution)/shard_map/all_to_all | solution.py:153
  63.0 0.0 collective-permute-done.2
  63.0 0.8 pad_maximum_fusion
  63.9 5.1 %all-to-all-done.3 = bf16[4,256,128]{2,1,0:T(8,128)(2,1)S(1)} async-done(((bf16[4,256,128]{2,1,0:T(8,128)(2,1)}), bf16[4,256,128]{2,1,0:T(8,128)(2,1)S(1)}, u32[]{:S(2)}, u32[]{:S(2)}) %all-to-all-start.3) | async-done | bytes 262176 | tf_op jit(solution)/shard_map/all_to_all | solution.py:153
  69.0 3.5 %all-to-all-start.4 = ((f32[4,256,128]{2,1,0:T(8,128)}), f32[4,256,128]{2,1,0:T(8,128)S(1)}, u32[]{:S(2)}, u32[]{:S(2)}) async-start(f32[4,256,128]{2,1,0:T(8,128)} %pad_maximum_fusion), calls=%async_computation.4 | async-start | bytes 1048576 | tf_op jit(solution)/shard_map/all_to_all | solution.py:156
  72.5 2.4 %collective-permute-start.3 = (f32[64,128]{1,0:T(8,128)S(1)}, f32[64,128]{1,0:T(8,128)S(1)}, u32[]{:S(2)}, u32[]{:S(2)}) collective-permute-start(f32[64,128]{1,0:T(8,128)S(1)} %slice_bitcast_fusion), channel_id=1, source_target_pairs={{4,0},{8,4},{12,8},{16,12},{20,16},{24,20},{28,24},{5,1},{9,5},{13... | collective-permute-start | bytes 98312 | tf_op jit(solution)/shard_map/ppermute | solution.py:16
  75.0 3.3 %collective-permute-done.3 = f32[64,128]{1,0:T(8,128)S(1)} collective-permute-done((f32[64,128]{1,0:T(8,128)S(1)}, f32[64,128]{1,0:T(8,128)S(1)}, u32[]{:S(2)}, u32[]{:S(2)}) %collective-permute-start.3) | collective-permute-done | bytes 32800 | tf_op jit(solution)/shard_map/ppermute | solution.py:16
  78.3 0.8 pad_maximum_fusion.1
  79.2 2.1 %all-to-all-done.4 = f32[4,256,128]{2,1,0:T(8,128)S(1)} async-done(((f32[4,256,128]{2,1,0:T(8,128)}), f32[4,256,128]{2,1,0:T(8,128)S(1)}, u32[]{:S(2)}, u32[]{:S(2)}) %all-to-all-start.4) | async-done | bytes 524320 | tf_op jit(solution)/shard_map/all_to_all | solution.py:156
  81.3 3.5 %all-to-all-start.5 = ((f32[4,256,128]{2,1,0:T(8,128)}), f32[4,256,128]{2,1,0:T(8,128)S(1)}, u32[]{:S(2)}, u32[]{:S(2)}) async-start(f32[4,256,128]{2,1,0:T(8,128)} %pad_maximum_fusion.1), calls=%async_computation.5 | async-start | bytes 1048576 | tf_op jit(solution)/shard_map/all_to_all | solution.py:157
  84.8 0.1 copy.11
  84.9 0.8 copy.15
  85.8 0.1 copy.14
  85.9 0.8 copy.16
  86.8 0.7 reduce_sum.58
  87.4 6.2 %all-to-all-done.5 = f32[4,256,128]{2,1,0:T(8,128)S(1)} async-done(((f32[4,256,128]{2,1,0:T(8,128)}), f32[4,256,128]{2,1,0:T(8,128)S(1)}, u32[]{:S(2)}, u32[]{:S(2)}) %all-to-all-start.5) | async-done | bytes 524320 | tf_op jit(solution)/shard_map/all_to_all | solution.py:157
  93.6 0.7 reduce_sum.59
  (33 shorter events, 0.2 us)
Async XLA Ops:
  0.6 9.7 %copy-start.2 = (bf16[256,128]{1,0:T(8,128)(2,1)S(1)}, bf16[256,128]{1,0:T(8,128)(2,1)}, u32[]{:S(2)}) copy-start(bf16[256,128]{1,0:T(8,128)(2,1)} %param.18) | copy-start | bytes 196612
  6.8 12.8 %copy-start = (bf16[256,512]{1,0:T(8,128)(2,1)S(1)}, bf16[256,512]{1,0:T(8,128)(2,1)}, u32[]{:S(2)}) copy-start(bf16[256,512]{1,0:T(8,128)(2,1)} %param.20) | copy-start | bytes 786436
  6.8 26.7 %collective-permute-start.1 = (bf16[64,128]{1,0:T(8,128)(2,1)S(1)}, bf16[64,128]{1,0:T(8,128)(2,1)S(1)}, u32[]{:S(2)}, u32[]{:S(2)}) collective-permute-start(bf16[64,128]{1,0:T(8,128)(2,1)S(1)} %slice_bitcast_fusion.2), channel_id=1, source_target_pairs={{0,4},{4,8},{8,12},{12,16},{16,20},{20,24},{24,28},{1,5},{5,9},{9,... | collective-permute-start | bytes 49160 | tf_op jit(solution)/shard_map/ppermute | solution.py:16
  16.1 17.9 %collective-permute-start = (bf16[64,128]{1,0:T(8,128)(2,1)S(1)}, bf16[64,128]{1,0:T(8,128)(2,1)S(1)}, u32[]{:S(2)}, u32[]{:S(2)}) collective-permute-start(bf16[64,128]{1,0:T(8,128)(2,1)S(1)} %slice_bitcast_fusion.3), channel_id=1, source_target_pairs={{0,4},{4,8},{8,12},{12,16},{16,20},{20,24},{24,28},{1,5},{5,9},{9,... | collective-permute-start | bytes 49160 | tf_op jit(solution)/shard_map/ppermute | solution.py:16
  20.5 3.7 %copy-start.8 = (s32[32]{0:T(128)S(1)}, s32[32]{0:T(128)}, u32[]{:S(2)}) copy-start(s32[32]{0:T(128)} %param.21) | copy-start | bytes 388
  20.6 9.5 %all-to-all-start.2 = ((bf16[256,4,128]{2,0,1:T(8,128)(2,1)}), bf16[256,4,128]{2,0,1:T(8,128)(2,1)S(1)}, u32[]{:S(2)}, u32[]{:S(2)}) async-start(bf16[256,4,128]{2,0,1:T(8,128)(2,1)} %copy.13), calls=%async_computation.2 | async-start | bytes 524288 | tf_op jit(solution)/shard_map/all_to_all | solution.py:76
  24.1 1.8 %copy-start.1 = (bf16[256,512]{1,0:T(8,128)(2,1)S(1)}, bf16[256,512]{1,0:T(8,128)(2,1)}, u32[]{:S(2)}) copy-start(bf16[256,512]{1,0:T(8,128)(2,1)} %param.17) | copy-start | bytes 786436
  24.1 19.4 %copy-start.11 = (pred[320]{0:T(512)(128)(4,1)}, pred[320]{0:T(512)(128)(4,1)S(1)}, u32[]{:S(2)}) copy-start(pred[320]{0:T(512)(128)(4,1)S(1)} %broadcast_compare_fusion.1) | copy-start | bytes 964
  24.2 19.4 %copy-start.9 = (pred[4]{0:T(512)(128)(4,1)}, pred[4]{0:T(512)(128)(4,1)S(1)}, u32[]{:S(2)}) copy-start(pred[4]{0:T(512)(128)(4,1)S(1)} %add_compare_fusion) | copy-start | bytes 16
  25.1 18.5 %copy-start.5 = (pred[128,320]{0,1:T(8,128)(4,1)}, pred[128,320]{0,1:T(8,128)(4,1)S(1)}, u32[]{:S(2)}) copy-start(pred[128,320]{0,1:T(8,128)(4,1)S(1)} %broadcast_compare_fusion) | copy-start | bytes 122884
  25.9 22.8 %copy-start.3 = (bf16[3,64,128]{2,1,0:T(8,128)(2,1)}, bf16[3,64,128]{2,1,0:T(8,128)(2,1)S(1)}, u32[]{:S(2)}) copy-start(bf16[3,64,128]{2,1,0:T(8,128)(2,1)S(1)} %slice.168) | copy-start | bytes 147460
  30.1 9.4 %all-to-all-start = ((bf16[256,4,128]{2,0,1:T(8,128)(2,1)}), bf16[256,4,128]{2,0,1:T(8,128)(2,1)S(1)}, u32[]{:S(2)}, u32[]{:S(2)}) async-start(bf16[256,4,128]{2,0,1:T(8,128)(2,1)} %copy.10), calls=%async_computation | async-start | bytes 524288 | tf_op jit(solution)/shard_map/all_to_all | solution.py:75
  34.0 14.7 %copy-start.6 = (bf16[64,128]{1,0:T(8,128)(2,1)}, bf16[64,128]{1,0:T(8,128)(2,1)S(1)}, u32[]{:S(2)}) copy-start(bf16[64,128]{1,0:T(8,128)(2,1)S(1)} %collective-permute-done) | copy-start | bytes 49156
  45.3 14.3 %all-to-all-start.1 = ((bf16[4,256,128]{2,1,0:T(8,128)(2,1)}), bf16[4,256,128]{2,1,0:T(8,128)(2,1)S(1)}, u32[]{:S(2)}, u32[]{:S(2)}) async-start(bf16[4,256,128]{2,1,0:T(8,128)(2,1)} %pad_maximum_fusion.4), calls=%async_computation.1 | async-start | bytes 524288 | tf_op jit(solution)/shard_map/all_to_all | solution.py:148
  51.4 5.1 %copy-start.10 = (pred[4]{0:T(512)(128)(4,1)S(1)}, pred[4]{0:T(512)(128)(4,1)}, u32[]{:S(2)}) copy-start(pred[4]{0:T(512)(128)(4,1)} %copy-done.9) | copy-start | bytes 16
  51.4 5.1 %copy-start.12 = (pred[320]{0:T(512)(128)(4,1)S(1)}, pred[320]{0:T(512)(128)(4,1)}, u32[]{:S(2)}) copy-start(pred[320]{0:T(512)(128)(4,1)} %copy-done.11) | copy-start | bytes 964
  53.2 3.4 %copy-start.4 = (bf16[3,64,128]{2,1,0:T(8,128)(2,1)S(1)}, bf16[3,64,128]{2,1,0:T(8,128)(2,1)}, u32[]{:S(2)}) copy-start(bf16[3,64,128]{2,1,0:T(8,128)(2,1)} %copy-done.3) | copy-start | bytes 147460
  53.2 3.4 %copy-start.7 = (bf16[64,128]{1,0:T(8,128)(2,1)S(1)}, bf16[64,128]{1,0:T(8,128)(2,1)}, u32[]{:S(2)}) copy-start(bf16[64,128]{1,0:T(8,128)(2,1)} %copy-done.6) | copy-start | bytes 49156
  53.2 9.8 %collective-permute-start.2 = (f32[64,128]{1,0:T(8,128)S(1)}, f32[64,128]{1,0:T(8,128)S(1)}, u32[]{:S(2)}, u32[]{:S(2)}) collective-permute-start(f32[64,128]{1,0:T(8,128)S(1)} %slice_bitcast_fusion.1), channel_id=1, source_target_pairs={{4,0},{8,4},{12,8},{16,12},{20,16},{24,20},{28,24},{5,1},{9,5},{13... | collective-permute-start | bytes 98312 | tf_op jit(solution)/shard_map/ppermute | solution.py:16
  59.6 9.4 %all-to-all-start.3 = ((bf16[4,256,128]{2,1,0:T(8,128)(2,1)}), bf16[4,256,128]{2,1,0:T(8,128)(2,1)S(1)}, u32[]{:S(2)}, u32[]{:S(2)}) async-start(bf16[4,256,128]{2,1,0:T(8,128)(2,1)} %pad_maximum_fusion.5), calls=%async_computation.3 | async-start | bytes 524288 | tf_op jit(solution)/shard_map/all_to_all | solution.py:153
  69.0 12.3 %all-to-all-start.4 = ((f32[4,256,128]{2,1,0:T(8,128)}), f32[4,256,128]{2,1,0:T(8,128)S(1)}, u32[]{:S(2)}, u32[]{:S(2)}) async-start(f32[4,256,128]{2,1,0:T(8,128)} %pad_maximum_fusion), calls=%async_computation.4 | async-start | bytes 1048576 | tf_op jit(solution)/shard_map/all_to_all | solution.py:156
  72.5 5.8 %collective-permute-start.3 = (f32[64,128]{1,0:T(8,128)S(1)}, f32[64,128]{1,0:T(8,128)S(1)}, u32[]{:S(2)}, u32[]{:S(2)}) collective-permute-start(f32[64,128]{1,0:T(8,128)S(1)} %slice_bitcast_fusion), channel_id=1, source_target_pairs={{4,0},{8,4},{12,8},{16,12},{20,16},{24,20},{28,24},{5,1},{9,5},{13... | collective-permute-start | bytes 98312 | tf_op jit(solution)/shard_map/ppermute | solution.py:16
  81.3 12.3 %all-to-all-start.5 = ((f32[4,256,128]{2,1,0:T(8,128)}), f32[4,256,128]{2,1,0:T(8,128)S(1)}, u32[]{:S(2)}, u32[]{:S(2)}) async-start(f32[4,256,128]{2,1,0:T(8,128)} %pad_maximum_fusion.1), calls=%async_computation.5 | async-start | bytes 1048576 | tf_op jit(solution)/shard_map/all_to_all | solution.py:157
